TPU v7x, 32 devices: a whole 2x2x4 slice. The times are simulated.
32 devices in a mesh: dp: 8 (over y, x, core), tensor: 4 (over z).
Axes of the slice: x: 2, y: 2, z: 4, core: 2. Of those that a mesh axis runs over, the one named last changes fastest.
Arguments:
- tokens: bfloat16 [8, 1024, 768], P('dp', 'tensor'), may hold values from -30 to 30
- segment_ids: int32 [8, 1024], P('dp'), may hold values from 0 to 3, never falling along the last dimension, each value on 1 to 512 neighbouring positions
- qkv_weight: bfloat16 [3, 768, 768], P(None, 'dp', 'tensor'), may hold values from -1 to 1
- out_weight: bfloat16 [768, 768], P('tensor', 'dp'), may hold values from -0.875 to 0.875
- in_weight: bfloat16 [768, 3072], P('dp', 'tensor'), may hold values from -0.21875 to 0.21875
- down_weight: bfloat16 [3072, 768], P('tensor', 'dp'), may hold values from -0.109375 to 0.109375
- qv_bias: bfloat16 [2, 4, 192], P(None, 'tensor', 'dp'), may hold values from -3 to 3
- hidden_bias: bfloat16 [4, 768], P('tensor', 'dp'), may hold values from -3 to 3
- norm_vectors: float32 [6, 768], P(None, ('dp', 'tensor')), may hold values from -2 to 2
- cotangent: bfloat16 [8, 1024, 768], P('dp', 'tensor'), may hold values from -6 to 6
Outputs:
- layer_out: bfloat16 [8, 1024, 768], P('dp', 'tensor')
- tokens_grad: bfloat16 [8, 1024, 768], P('dp', 'tensor')
- qkv_grad: float32 [3, 768, 768], P(None, 'dp', 'tensor')
- out_grad: float32 [768, 768], P('tensor', 'dp')
- in_grad: float32 [768, 3072], P('dp', 'tensor')
- down_grad: float32 [3072, 768], P('tensor', 'dp')
- qv_bias_grad: float32 [2, 4, 192], P(None, 'tensor', 'dp')
- hidden_bias_grad: float32 [4, 768], P('tensor', 'dp')
- vectors_grad: float32 [6, 768], P(None, ('dp', 'tensor'))
Inputs may be any that keep to these rules, and one draw needn't show every extreme that they name: `segment_ids`: segment ids never fall along a sequence; each document holds 1 to 512 tokens, one exactly 512.
All inputs are finite; a program needn't handle non-finite values.
Results may differ from a plain program's by a relative error of at most 0.028.
The roundings to bfloat16 on the way count: a program that leaves them out, or rounds other values in their place, can miss the bound.
Values may be sent and summed in bfloat16 or wider, within the bound.
A program may use at most 128 MiB of HBM per device.

v0:
```python
import jax
import jax.numpy as jnp
from jax import lax
from jax.sharding import PartitionSpec as P

DH = 64


EPS = 1e-05
MASKED = -1e30


def layer_norm(summed, gain, shift):
    center = summed - jnp.mean(summed, -1, keepdims=True)
    inv_std = lax.rsqrt(jnp.mean(center * center, -1, keepdims=True) + EPS)
    normed = center * inv_std
    return (normed * gain + shift, normed, inv_std)


def norm_back(upstream, normed, inv_std, gain):
    scaled = upstream * gain
    return inv_std * (
        scaled
        - jnp.mean(scaled, -1, keepdims=True)
        - normed * jnp.mean(scaled * normed, -1, keepdims=True)
    )


def gelu_parts(inputs):
    cdf_part = 0.5 * (1.0 + lax.erf(inputs * 0.7071067811865476))
    return (
        inputs * cdf_part,
        cdf_part + inputs * jnp.exp(-0.5 * inputs * inputs) * 0.3989422804014327,
    )


def local(
    tokens,
    segment_ids,
    qkv_weight,
    out_weight,
    in_weight,
    down_weight,
    qv_bias,
    hidden_bias,
    norm_vectors,
    cotangent,
):
    vector_rows = lax.all_gather(norm_vectors, ("dp", "tensor"), axis=1, tiled=True)
    qkv_full, out_full, in_full, down_full, qv_full, hidden_full = (
        lax.all_gather(qkv_weight, "dp", axis=1, tiled=True),
        lax.all_gather(out_weight, "dp", axis=1, tiled=True),
        lax.all_gather(in_weight, "dp", axis=0, tiled=True),
        lax.all_gather(down_weight, "dp", axis=1, tiled=True),
        lax.all_gather(qv_bias, "dp", axis=2, tiled=True),
        lax.all_gather(hidden_bias, "dp", axis=1, tiled=True),
    )
    seq_count = tokens.shape[0]
    full_tokens = lax.all_gather(tokens, "tensor", axis=1, tiled=True)
    length = full_tokens.shape[1]
    local_width = qkv_full.shape[2]
    heads_here = local_width // DH
    score_scale = DH ** (-0.5)
    block_rows = min(512, length)
    block_count = length // block_rows
    head_shape = (seq_count, length, heads_here, DH)
    projected = jnp.einsum(
        "bld,cde->cble", full_tokens, qkv_full, preferred_element_type=jnp.float32
    )
    queries = (projected[0] + qv_full[0, 0]).astype(jnp.bfloat16).reshape(head_shape)
    key_rows = projected[1].astype(jnp.bfloat16).reshape(head_shape)
    value_rows = (projected[2] + qv_full[1, 0]).astype(jnp.bfloat16).reshape(head_shape)

    def block_scores(block_index):
        row_start = block_index * block_rows
        query_block = lax.dynamic_slice_in_dim(queries, row_start, block_rows, 1)
        segment_block = lax.dynamic_slice_in_dim(segment_ids, row_start, block_rows, 1)
        scores = (
            jnp.einsum("bqhd,bkhd->bhqk", query_block, key_rows, preferred_element_type=jnp.float32)
            * score_scale
        )
        allowed = segment_block[:, None, :, None] == segment_ids[:, None, None, :]
        return (jnp.where(allowed, scores, MASKED), query_block)

    def attend(block_index):
        scores, query_block = block_scores(block_index)
        row_max = jnp.max(scores, -1, keepdims=True)
        shifted = jnp.exp(scores - row_max)
        row_total = jnp.sum(shifted, -1, keepdims=True)
        attn_probs = (shifted / row_total).astype(jnp.bfloat16)
        context = jnp.einsum(
            "bhqk,bkhd->bqhd", attn_probs, value_rows, preferred_element_type=jnp.float32
        ).astype(jnp.bfloat16)
        return (context, (row_max + jnp.log(row_total))[..., 0])

    contexts, log_sums = lax.map(attend, jnp.arange(block_count))
    context_rows = jnp.moveaxis(contexts, 0, 1).reshape(seq_count, length, local_width)
    attn_part = jnp.einsum(
        "ble,ed->bld", context_rows, out_full, preferred_element_type=jnp.float32
    )
    attn_sum = lax.psum_scatter(
        attn_part.astype(jnp.bfloat16), "tensor", scatter_dimension=1, tiled=True
    ).astype(jnp.float32)
    first_sum = tokens.astype(jnp.float32) + attn_sum + vector_rows[0]
    normed_one, unit_one, inv_one = layer_norm(first_sum, vector_rows[1], vector_rows[2])
    normed_full = lax.all_gather(normed_one.astype(jnp.bfloat16), "tensor", axis=1, tiled=True)
    hidden_pre = (
        jnp.einsum("bld,df->blf", normed_full, in_full, preferred_element_type=jnp.float32)
        + hidden_full[0]
    )
    activated, gelu_slope = gelu_parts(hidden_pre)
    act_low = activated.astype(jnp.bfloat16)
    mlp_part = jnp.einsum("blf,fd->bld", act_low, down_full, preferred_element_type=jnp.float32)
    mlp_sum = lax.psum_scatter(
        mlp_part.astype(jnp.bfloat16), "tensor", scatter_dimension=1, tiled=True
    ).astype(jnp.float32)
    second_sum = normed_one + mlp_sum + vector_rows[3]
    normed_two, unit_two, inv_two = layer_norm(second_sum, vector_rows[4], vector_rows[5])
    layer_out = normed_two.astype(jnp.bfloat16)
    upstream = cotangent.astype(jnp.float32)
    grad_second = norm_back(upstream, unit_two, inv_two, vector_rows[4])
    grad_mlp_full = lax.all_gather(grad_second.astype(jnp.bfloat16), "tensor", axis=1, tiled=True)
    down_grad = jnp.einsum(
        "blf,bld->fd", act_low, grad_mlp_full, preferred_element_type=jnp.float32
    )
    grad_hidden = (
        jnp.einsum("bld,fd->blf", grad_mlp_full, down_full, preferred_element_type=jnp.float32)
        * gelu_slope
    )
    hidden_low = grad_hidden.astype(jnp.bfloat16)
    hidden_grad = jnp.sum(grad_hidden, (0, 1))[None]
    in_grad = jnp.einsum("bld,blf->df", normed_full, hidden_low, preferred_element_type=jnp.float32)
    back_part = jnp.einsum("blf,df->bld", hidden_low, in_full, preferred_element_type=jnp.float32)
    grad_normed = grad_second + lax.psum_scatter(
        back_part.astype(jnp.bfloat16), "tensor", scatter_dimension=1, tiled=True
    ).astype(jnp.float32)
    grad_first = norm_back(grad_normed, unit_one, inv_one, vector_rows[1])
    grad_attn_full = lax.all_gather(grad_first.astype(jnp.bfloat16), "tensor", axis=1, tiled=True)
    out_grad = jnp.einsum(
        "ble,bld->ed", context_rows, grad_attn_full, preferred_element_type=jnp.float32
    )
    grad_context = jnp.einsum(
        "bld,ed->ble", grad_attn_full, out_full, preferred_element_type=jnp.float32
    ).astype(jnp.bfloat16)
    grad_heads = grad_context.reshape(head_shape)
    row_delta = jnp.sum(
        grad_heads.astype(jnp.float32) * context_rows.reshape(head_shape).astype(jnp.float32), -1
    )

    def backward_block(running, block_index):
        key_grad, value_grad = running
        scores, query_block = block_scores(block_index)
        row_start = block_index * block_rows
        grad_block = lax.dynamic_slice_in_dim(grad_heads, row_start, block_rows, 1)
        delta_block = lax.dynamic_slice_in_dim(row_delta, row_start, block_rows, 1)
        probs_again = jnp.exp(scores - log_sums[block_index][..., None])
        probs_low = probs_again.astype(jnp.bfloat16)
        value_grad = value_grad + jnp.einsum(
            "bhqk,bqhd->bkhd", probs_low, grad_block, preferred_element_type=jnp.float32
        )
        grad_probs = jnp.einsum(
            "bqhd,bkhd->bhqk", grad_block, value_rows, preferred_element_type=jnp.float32
        )
        grad_scores = (
            probs_again * (grad_probs - jnp.transpose(delta_block, (0, 2, 1))[..., None])
        ).astype(jnp.bfloat16)
        query_grad = (
            jnp.einsum("bhqk,bkhd->bqhd", grad_scores, key_rows, preferred_element_type=jnp.float32)
            * score_scale
        )
        key_grad = (
            key_grad
            + jnp.einsum(
                "bhqk,bqhd->bkhd", grad_scores, query_block, preferred_element_type=jnp.float32
            )
            * score_scale
        )
        return ((key_grad, value_grad), query_grad)

    zero_heads = jnp.zeros(head_shape, jnp.float32)
    (key_grad, value_grad), query_grads = lax.scan(
        backward_block, (zero_heads, zero_heads), jnp.arange(block_count)
    )
    query_grad = jnp.moveaxis(query_grads, 0, 1).reshape(seq_count, length, local_width)
    key_grad = key_grad.reshape(seq_count, length, local_width)
    value_grad = value_grad.reshape(seq_count, length, local_width)
    bias_grad = jnp.stack([jnp.sum(query_grad, (0, 1)), jnp.sum(value_grad, (0, 1))])[:, None, :]
    grads_low = jnp.stack([query_grad, key_grad, value_grad]).astype(jnp.bfloat16)
    qkv_grad = jnp.einsum(
        "bld,cble->cde", full_tokens, grads_low, preferred_element_type=jnp.float32
    )
    token_part = jnp.einsum(
        "cble,cde->bld", grads_low, qkv_full, preferred_element_type=jnp.float32
    )
    tokens_grad = (
        grad_first
        + lax.psum_scatter(
            token_part.astype(jnp.bfloat16), "tensor", scatter_dimension=1, tiled=True
        ).astype(jnp.float32)
    ).astype(jnp.bfloat16)
    qkv_shard, out_shard, in_shard, down_shard, bias_shard, hidden_shard = (
        lax.psum_scatter(qkv_grad, "dp", scatter_dimension=1, tiled=True),
        lax.psum_scatter(out_grad, "dp", scatter_dimension=1, tiled=True),
        lax.psum_scatter(in_grad, "dp", scatter_dimension=0, tiled=True),
        lax.psum_scatter(down_grad, "dp", scatter_dimension=1, tiled=True),
        lax.psum_scatter(bias_grad, "dp", scatter_dimension=2, tiled=True),
        lax.psum_scatter(hidden_grad, "dp", scatter_dimension=1, tiled=True),
    )
    vector_grad = jnp.stack(
        [
            jnp.sum(grad_first, (0, 1)),
            jnp.sum(grad_normed * unit_one, (0, 1)),
            jnp.sum(grad_normed, (0, 1)),
            jnp.sum(grad_second, (0, 1)),
            jnp.sum(upstream * unit_two, (0, 1)),
            jnp.sum(upstream, (0, 1)),
        ]
    )
    vectors_grad = lax.psum_scatter(vector_grad, ("dp", "tensor"), scatter_dimension=1, tiled=True)
    return (
        layer_out,
        tokens_grad,
        qkv_shard,
        out_shard,
        in_shard,
        down_shard,
        bias_shard,
        hidden_shard,
        vectors_grad,
    )


def solution(mesh):
    return jax.shard_map(
        local,
        mesh=mesh,
        in_specs=(
            P("dp", "tensor", None),
            P("dp", None),
            P(None, "dp", "tensor"),
            P("tensor", "dp"),
            P("dp", "tensor"),
            P("tensor", "dp"),
            P(None, "tensor", "dp"),
            P("tensor", "dp"),
            P(None, ("dp", "tensor")),
            P("dp", "tensor", None),
        ),
        out_specs=(
            P("dp", "tensor", None),
            P("dp", "tensor", None),
            P(None, "dp", "tensor"),
            P("tensor", "dp"),
            P("dp", "tensor"),
            P("tensor", "dp"),
            P(None, "tensor", "dp"),
            P("tensor", "dp"),
            P(None, ("dp", "tensor")),
        ),
        check_vma=False,
    )
```

profile of v0, /device:TPU:10, one launch (start us, length us, event | category | flops | bytes accessed | tf_op | source)
XLA Modules:
  0.0 622.0 jit_solution(14623670875500155624)
XLA Ops:
  10.5 9.2 %all_gather.35 = bf16[2,1,192]{1,0,2:T(2,128)(2,1)S(1)} all-gather(bf16[2,1,24]{1,0,2:T(2,128)(2,1)S(1)} %copy.43), channel_id=1, replica_groups=mesh['dp'=8,'tensor'=4] {'dp'}, dimensions={2}, use_global_device_ids=true | all-gather | bytes 864 | tf_op jit(solution)/shard_map/all_gather | solution.py:55
  22.0 8.6 %all_gather.36 = bf16[192,768]{0,1:T(8,128)(2,1)S(1)} all-gather(bf16[192,96]{0,1:T(8,128)(2,1)S(1)} %copy.45), channel_id=1, replica_groups=mesh['dp'=8,'tensor'=4] {'dp'}, dimensions={1}, use_global_device_ids=true | all-gather | bytes 331776 | tf_op jit(solution)/shard_map/all_gather | solution.py:52
  30.6 14.3 %all_gather.33 = bf16[3,768,192]{2,0,1:T(4,128)(2,1)} all-gather(bf16[3,96,192]{2,0,1:T(4,128)(2,1)S(1)} %copy.41), channel_id=1, replica_groups=mesh['dp'=8,'tensor'=4] {'dp'}, dimensions={1}, use_global_device_ids=true | all-gather | bytes 995328 | tf_op jit(solution)/shard_map/all_gather | solution.py:51
  44.9 2.7 all-gather.8.cloned.1.call-done
  47.7 3.4 convolution_bitcast_fusion
  52.1 14.2 %while.27 = (s32[]{:T(128)}, bf16[2,1,512,3,64]{2,4,3,1,0:T(8,128)(2,1)S(1)}, f32[2,1,3,512]{3,2,1,0:T(4,128)S(1)}, s32[2]{0:T(128)S(1)}, s32[1,1024]{1,0:T(1,12...) while((s32[]{:T(128)}, ...), condition=%wide.region_3.4_spmd, body=%wide.region_0.3_spmd.sunk | while | flops 422148608 | bytes 23793892 | solution.py:96
  55.1 1.8 fusion.139
  57.0 2.2 fusion.140
  62.2 1.8 fusion.139
  64.1 2.2 fusion.140
  67.0 1.8 fusion.69
  69.5 60.8 %all-gather = f32[32,24,6]{1,2,0:T(8,128)S(1)} all-gather(f32[1,24,6]{1,2,0:T(8,128)S(1)} %bitcast.252), channel_id=1, replica_groups=mesh['dp'=8,'tensor'=4] {'dp','tensor'}, dimensions={0}, use_global_device_ids=true | all-gather | bytes 19008 | tf_op jit(solution)/shard_map/all_gather | solution.py:49
  133.5 2.0 fusion.89
  137.7 17.3 %all-reduce = bf16[768]{0:T(1024)(128)(2,1)S(1)} all-reduce(bf16[768]{0:T(1024)(128)(2,1)S(1)} %dynamic-update-slice), channel_id=1, replica_groups=mesh['dp'=8,'tensor'=4] {'dp'}, use_global_device_ids=true, to_apply=%add | all-reduce | flops 768 | bytes 3072
  154.9 21.9 %all-gather.10.cloned.1.call-done = bf16[1,1024,768]{2,1,0:T(8,128)(2,1)} async-done(((bf16[1,256,768]{2,1,0:T(8,128)(2,1)}), bf16[1,1024,768]{2,1,0:T(8,128)(2,1)}) %all-gather.10.cloned.1.call-update) | async-done | bytes 1572880 | tf_op jit(solution)/shard_map/all_gather | solution.py:106
  176.9 5.4 multiply_convert_fusion.1
  182.2 20.0 %all-gather.14.cloned.1.call-done = bf16[768,768]{0,1:T(8,128)(2,1)} async-done(((bf16[768,96]{0,1:T(8,128)(2,1)}), bf16[768,768]{0,1:T(8,128)(2,1)}) %all-gather.14.cloned.1.call-update) | async-done | bytes 1179664 | tf_op jit(solution)/shard_map/all_gather | solution.py:54
  202.2 4.4 fusion.70
  206.7 34.2 %reduce-scatter.20.cloned.1.call-done = bf16[1,256,768]{2,1,0:T(8,128)(2,1)} async-done(((bf16[1,1024,768]{2,1,0:T(8,128)(2,1)}), bf16[1,256,768]{2,1,0:T(8,128)(2,1)}) %reduce-scatter.20.cloned.1.call-update) | async-done | bytes 393232 | tf_op jit(solution)/shard_map/reduce_scatter | solution.py:114
  243.6 2.2 fusion.97
  245.9 36.3 %all-gather.16.cloned.1.call-done = bf16[1,1024,768]{2,1,0:T(8,128)(2,1)} async-done(((bf16[1,256,768]{2,1,0:T(8,128)(2,1)}), bf16[1,1024,768]{2,1,0:T(8,128)(2,1)}) %all-gather.16.cloned.1.call-update) | async-done | bytes 1572880 | tf_op jit(solution)/shard_map/all_gather | solution.py:122
  282.2 5.5 fusion.104
  288.9 2.6 fusion.71
  291.5 33.9 %reduce-scatter.22.cloned.1.call-done = bf16[1,256,768]{2,1,0:T(8,128)(2,1)} async-done(((bf16[1,1024,768]{2,1,0:T(8,128)(2,1)}), bf16[1,256,768]{2,1,0:T(8,128)(2,1)}) %reduce-scatter.22.cloned.1.call-update) | async-done | bytes 393232 | tf_op jit(solution)/shard_map/reduce_scatter | solution.py:134
  325.4 2.2 multiply_reduce_fusion
  327.6 2.0 fusion.96
  332.6 35.1 %all-gather.18.cloned.1.call-done = bf16[1,1024,768]{2,1,0:T(8,128)(2,1)} async-done(((bf16[1,256,768]{2,1,0:T(8,128)(2,1)}), bf16[1,1024,768]{2,1,0:T(8,128)(2,1)}) %all-gather.18.cloned.1.call-update) | async-done | bytes 1572880 | tf_op jit(solution)/shard_map/all_gather | solution.py:138
  367.7 2.2 fusion.75
  369.9 1.6 fusion.72
  371.9 26.3 %while.28 = (s32[]{:T(128)}, f32[1,1024,3,64]{1,3,2,0:T(8,128)S(1)}, f32[1,1024,3,64]{1,3,2,0:T(8,128)}, f32[2,1,512,3,64]{2,4,3,1,0:T(8,128)}, s32[2]{0:T(128)S...) while((s32[]{:T(128)}, ...), condition=%wide.region_17.18_spmd.clone, body=%wide.region_16.17_spmd.clone.sunk | while | flops 1023967232 | bytes 49703404 | solution.py:181
  377.4 1.9 fusion.153
  379.3 2.6 multiply_convert_fusion.3
  390.5 1.9 fusion.153
  392.5 2.6 multiply_convert_fusion.3
  402.2 2.4 fusion.65
  404.6 2.9 copy.51
  407.5 2.9 reshape.545
  410.5 4.5 fusion.68
  415.0 2.8 fusion.55
  419.3 4.3 fusion.58
  425.9 40.9 %all-reduce.2 = f32[6,768]{1,0:T(8,128)S(1)} all-reduce(f32[6,768]{1,0:T(8,128)S(1)} %stack.52), channel_id=12, replica_groups=mesh['dp'=8,'tensor'=4] {'dp','tensor'}, use_global_device_ids=true, to_apply=%region_34.35.clone | all-reduce | flops 4608 | bytes 36864
  467.7 10.6 %all-reduce.1 = f32[2,1,192]{2,1,0:T(1,128)S(1)} all-reduce(f32[2,1,192]{2,1,0:T(1,128)S(1)} %broadcast_in_dim.70), channel_id=10, replica_groups=mesh['dp'=8,'tensor'=4] {'dp'}, use_global_device_ids=true, to_apply=%region_25.26.clone | all-reduce | flops 384 | bytes 3072
  479.0 1.6 copy.54
  480.6 5.4 reduce-scatter.30.cloned.1.call-done
  487.9 34.3 %reduce-scatter.24.cloned.1.call-done = bf16[1,256,768]{2,1,0:T(8,128)(2,1)} async-done(((bf16[1,1024,768]{2,1,0:T(8,128)(2,1)}), bf16[1,256,768]{2,1,0:T(8,128)(2,1)}) %reduce-scatter.24.cloned.1.call-update) | async-done | bytes 393232 | tf_op jit(solution)/shard_map/reduce_scatter | solution.py:197
  522.2 1.8 add_convert_fusion
  524.0 44.6 %reduce-scatter.28.cloned.1.call-done = f32[768,96]{0,1:T(8,128)} async-done(((f32[768,768]{0,1:T(8,128)}), f32[768,96]{0,1:T(8,128)}) %reduce-scatter.28.cloned.1.call-update) | async-done | bytes 294928 | tf_op jit(solution)/shard_map/reduce_scatter | solution.py:205
  568.6 46.1 %reduce-scatter.26.cloned.1.call-done = f32[96,768]{1,0:T(8,128)} async-done(((f32[768,768]{1,0:T(8,128)}), f32[96,768]{1,0:T(8,128)}) %reduce-scatter.26.cloned.1.call-update) | async-done | bytes 294928 | tf_op jit(solution)/shard_map/reduce_scatter | solution.py:204
  (216 shorter events, 46.0 us)
Async XLA Ops:
  8.0 39.7 %all-gather.8.cloned.1.call-start = ((), (), s32[]{:S(2)}) async-start(), calls=%async_computation.9 | async-start | bytes 1966080 | tf_op jit(solution)/shard_map/all_gather | solution.py:59
  8.7 122.3 %reduce-scatter.18.cloned.1.call-start = ((), (), s32[]{:S(2)}) async-start(), calls=%async_computation.10 | async-start | bytes 1966080 | tf_op jit(solution)/shard_map/reduce_scatter | solution.py:101
  55.1 1.8 copy-start.12
  62.2 1.8 copy-start.12
  66.9 2.5 copy-start.28
  67.0 64.0 %copy-start = (bf16[1,256,768]{2,1,0:T(8,128)(2,1)S(1)}, bf16[1,256,768]{2,1,0:T(8,128)(2,1)}, u32[]{:S(2)}) copy-start(bf16[1,256,768]{2,1,0:T(8,128)(2,1)} %param.14) | copy-start | bytes 1179652
  68.8 67.4 %copy-start.30 = (u32[32]{0:T(128)S(1)}, u32[32]{0:T(128)}, u32[]{:S(2)}) copy-start(u32[32]{0:T(128)} %constant.82) | copy-start | bytes 388
  68.8 68.6 %copy-start.35 = (bf16[1,96]{1,0:T(2,128)(2,1)S(1)}, bf16[1,96]{1,0:T(2,128)(2,1)}, u32[]{:S(2)}) copy-start(bf16[1,96]{1,0:T(2,128)(2,1)} %param.21) | copy-start | bytes 580
  68.8 86.1 %all-gather.12.cloned.1.call-start = ((), (), s32[]{:S(2)}) async-start(), calls=%async_computation.12 | async-start | bytes 1327104 | tf_op jit(solution)/shard_map/all_gather | solution.py:53
  69.4 107.5 %all-gather.10.cloned.1.call-start = ((), (), s32[]{:S(2)}) async-start(), calls=%async_computation.11 | async-start | bytes 1966080 | tf_op jit(solution)/shard_map/all_gather | solution.py:106
  131.0 111.6 %copy-start.19 = (f32[768]{0:T(1024)}, f32[768]{0:T(1024)S(1)}, u32[]{:S(2)}) copy-start(f32[768]{0:T(1024)S(1)} %get-tuple-element.207) | copy-start | bytes 9220
  133.5 107.5 %copy-start.20 = (f32[256]{0:T(256)}, f32[256]{0:T(256)S(1)}, u32[]{:S(2)}) copy-start(f32[256]{0:T(256)S(1)} %add_rsqrt_fusion.1) | copy-start | bytes 3076
  135.5 66.7 %all-gather.14.cloned.1.call-start = ((), (), s32[]{:S(2)}) async-start(), calls=%async_computation.13 | async-start | bytes 1327104 | tf_op jit(solution)/shard_map/all_gather | solution.py:54
  136.1 104.9 %reduce-scatter.20.cloned.1.call-start = ((), (), s32[]{:S(2)}) async-start(), calls=%async_computation.14 | async-start | bytes 1966080 | tf_op jit(solution)/shard_map/reduce_scatter | solution.py:114
  154.9 27.3 %copy-start.29 = (f32[768]{0:T(1024)}, f32[768]{0:T(1024)S(1)}, u32[]{:S(2)}) copy-start(f32[768]{0:T(1024)S(1)} %convert_element_type.206) | copy-start | bytes 9220
  202.2 38.7 %copy-start.1 = (bf16[1,256,768]{2,1,0:T(8,128)(2,1)S(1)}, bf16[1,256,768]{2,1,0:T(8,128)(2,1)}, u32[]{:S(2)}) copy-start(bf16[1,256,768]{2,1,0:T(8,128)(2,1)} %reduce-scatter.18.cloned.1.call-done) | copy-start | bytes 1179652
  206.7 35.9 %copy-start.5 = (bf16[1,256,768]{2,1,0:T(8,128)(2,1)S(1)}, bf16[1,256,768]{2,1,0:T(8,128)(2,1)}, u32[]{:S(2)}) copy-start(bf16[1,256,768]{2,1,0:T(8,128)(2,1)} %param.23) | copy-start | bytes 1179652
  206.7 75.5 %all-gather.16.cloned.1.call-start = ((), (), s32[]{:S(2)}) async-start(), calls=%async_computation.15 | async-start | bytes 1966080 | tf_op jit(solution)/shard_map/all_gather | solution.py:122
  245.8 79.6 %reduce-scatter.22.cloned.1.call-start = ((), (), s32[]{:S(2)}) async-start(), calls=%async_computation.16 | async-start | bytes 1966080 | tf_op jit(solution)/shard_map/reduce_scatter | solution.py:134
  282.2 6.7 %copy-start.34 = (bf16[768,768]{1,0:T(8,128)(2,1)S(1)}, bf16[768,768]{1,0:T(8,128)(2,1)}, u32[]{:S(2)}) copy-start(bf16[768,768]{1,0:T(8,128)(2,1)} %all-gather.12.cloned.1.call-done) | copy-start | bytes 3538948
  287.7 1.2 copy-start.37
  291.5 76.2 %all-gather.18.cloned.1.call-start = ((), (), s32[]{:S(2)}) async-start(), calls=%async_computation.17 | async-start | bytes 1966080 | tf_op jit(solution)/shard_map/all_gather | solution.py:138
  329.6 2.0 copy-start.27
  331.3 93.1 %reduce-scatter.34.cloned.1.call-start = ((), (), s32[]{:S(2)}) async-start(), calls=%async_computation.23 | async-start | bytes 442368
  332.5 146.4 %reduce-scatter.32.cloned.1.call-start = ((), (), s32[]{:S(2)}) async-start(), calls=%async_computation.22 | async-start | bytes 884736
  367.7 2.2 copy-start.4
  371.7 114.4 %reduce-scatter.30.cloned.1.call-start = ((), (), s32[]{:S(2)}) async-start(), calls=%async_computation.21 | async-start | bytes 2211840
  371.9 3.9 copy-start.16
  377.4 2.0 copy-start.13
  379.3 2.6 copy-start.10
  383.1 2.0 copy-start.17
  385.1 3.9 copy-start.16
  390.5 2.0 copy-start.13
  392.5 2.6 copy-start.10
  396.2 2.0 copy-start.17
  398.2 2.3 copy-start.11
  400.5 1.7 copy-start.31
  410.4 4.6 copy-start.33
  410.4 4.6 copy-start.36
  410.4 111.8 %reduce-scatter.24.cloned.1.call-start = ((), (), s32[]{:S(2)}) async-start(), calls=%async_computation.18 | async-start | bytes 1966080 | tf_op jit(solution)/shard_map/reduce_scatter | solution.py:197
  415.0 153.6 %reduce-scatter.28.cloned.1.call-start = ((), (), s32[]{:S(2)}) async-start(), calls=%async_computation.20 | async-start | bytes 2654208 | tf_op jit(solution)/shard_map/reduce_scatter | solution.py:205
  417.9 1.4 copy-start.32
  417.9 196.8 %reduce-scatter.26.cloned.1.call-start = ((), (), s32[]{:S(2)}) async-start(), calls=%async_computation.19 | async-start | bytes 2654208 | tf_op jit(solution)/shard_map/reduce_scatter | solution.py:204
  423.6 2.2 copy-start.25
  423.6 2.2 copy-start.26
  423.6 2.3 copy-start.24
  423.6 2.3 copy-start.23
  423.6 98.6 %copy-start.3 = (f32[1,256,768]{2,1,0:T(8,128)S(1)}, f32[1,256,768]{2,1,0:T(8,128)}, u32[]{:S(2)}) copy-start(f32[1,256,768]{2,1,0:T(8,128)} %copy-done.2) | copy-start | bytes 2359300
  (13 other events, 12.0 us)
Sparse Core Ops, SparseCore 0:
  10.4 37.2 all-gather.7
  68.9 35.1 reduce-scatter.17
  206.8 34.0 reduce-scatter.19
  291.6 33.7 reduce-scatter.21
Sparse Core Ops, SparseCore 1:
  71.2 23.6 all-gather.11
  135.6 41.2 all-gather.9
  178.6 23.5 all-gather.13
  245.9 36.2 all-gather.15
  331.4 36.2 all-gather.17
  370.7 33.6 reduce-scatter.33
  407.4 35.1 reduce-scatter.31
  445.9 40.1 reduce-scatter.29
  488.2 34.0 reduce-scatter.23
  526.2 42.4 reduce-scatter.27
  572.4 42.2 reduce-scatter.25
where the time goes:
time: 625 us; the launch traced here: 622 us
  waiting for transfers between devices  317 us (51%)
  blocking collectives  162 us (26%)
  matrix products  62.8 us (10%)
  local copies, waits for them, and re-layouts  30.5 us (5%)
  other arithmetic  25.1 us (4%)
  between operations  17.5 us (3%)
  loops' own time  6.82 us (1%)
    unnamed x3, blocking collectives  68.8 us
    all_gather x1, blocking collectives, local(): lax.all_gather(norm_vectors, ('dp', 'tensor'), axis=1, tiled=True)  60.8 us
    reduce_scatter x1, waiting for transfers between devices, local(): lax.psum_scatter(in_grad, 'dp', scatter_dimension=0, tiled=True)  46.1 us
    reduce_scatter x1, waiting for transfers between devices, local(): lax.psum_scatter(down_grad, 'dp', scatter_dimension=1, tiled=True)  44.6 us
    all_gather x1, waiting for transfers between devices, local(): lax.all_gather(grad_second.astype(jnp.bfloat16), 'tensor', axis=1, tiled=...  36.3 us
    all_gather x1, waiting for transfers between devices, local(): lax.all_gather(grad_first.astype(jnp.bfloat16), 'tensor', axis=1, tiled=T...  35.1 us
    reduce_scatter x1, waiting for transfers between devices, local(): lax.psum_scatter(token_part.astype(jnp.bfloat16), 'tensor', scatter_dimen...  34.3 us
    reduce_scatter x1, waiting for transfers between devices, local(): lax.psum_scatter(mlp_part.astype(jnp.bfloat16), 'tensor', scatter_dimensi...  34.2 us
  transfers between devices with their start and end apart: 15, of which 11 were waited for; matrix products, arithmetic and copies ran while one was open for 11% of the time, Pallas kernels for 0%

commit v1 on v0

v1 whole, which is shorter than its diff:
```python
import functools
import itertools
import jax
import jax.numpy as jnp
from jax import lax
from jax.experimental import pallas as pl
from jax.experimental.pallas import tpu as pltpu
from jax.sharding import PartitionSpec as P

DH = 64


EPS = 1e-05
MASKED = -1e30
MESH_ID = pl.DeviceIdType.MESH


def remote(src, dst, send_sem, recv_sem, where):
    return pltpu.make_async_remote_copy(
        src_ref=src, dst_ref=dst, send_sem=send_sem, recv_sem=recv_sem,
        device_id=where, device_id_type=MESH_ID)


def line_gather(n, pieces, x, out, send, recv, own):
    me = lax.axis_index("tensor")
    right, left = {"tensor": me + 1}, {"tensor": me - 1}

    def copy(way, step, c, shard, to):
        src = x.at[c] if step == 0 else out.at[shard, c]
        return remote(src, out.at[shard, c], send.at[way, step, c], recv.at[way, step, c], to)

    def landed(way, step, c, shard):
        to = right if way == 0 else left
        remote(out.at[shard, c], out.at[shard, c], send.at[way, step, c], recv.at[way, step, c], to).wait_recv()

    def stage(step):
        if step == 0:
            pltpu.make_async_copy(x, out.at[me], own).start()
        for c in range(pieces):
            if step > 0:
                pl.when(me - step >= 0)(lambda: landed(0, step - 1, c, me - step))
                pl.when(me + step <= n - 1)(lambda: landed(1, step - 1, c, me + step))
            if step < n - 1:
                pl.when((me < n - 1) & (me - step >= 0))(lambda: copy(0, step, c, me - step, right).start())
                pl.when((me > 0) & (me + step <= n - 1))(lambda: copy(1, step, c, me + step, left).start())

    def finish():
        pltpu.make_async_copy(x, out.at[me], own).wait()
        for step in range(n - 1):
            for c in range(pieces):
                pl.when((me < n - 1) & (me - step >= 0))(lambda: copy(0, step, c, me - step, right).wait_send())
                pl.when((me > 0) & (me + step <= n - 1))(lambda: copy(1, step, c, me + step, left).wait_send())

    return [functools.partial(stage, s) for s in range(n)] + [finish]


def line_scatter(n, pieces, p, out, got, acc, send, recv):
    me = lax.axis_index("tensor")
    right, left = {"tensor": me + 1}, {"tensor": me - 1}

    def copy(way, t, c):
        return remote(acc.at[way, t, c], got.at[way, t, c], send.at[way, t, c], recv.at[way, t, c],
                      right if way == 0 else left)

    def push(way, t, c, d):
        first = me == 0 if way == 0 else me == n - 1

        @pl.when(first)
        def _():
            acc[way, t, c] = p[d, c]

        @pl.when(jnp.logical_not(first))
        def _():
            copy(way, t, c).wait_recv()
            acc[way, t, c] = (p[d, c].astype(jnp.float32) + got[way, t, c].astype(jnp.float32)).astype(acc.dtype)

        copy(way, t, c).start()

    def stage(t):
        for c in range(pieces):
            pl.when(n - 1 - t > me)(lambda: push(0, t, c, n - 1 - t))
            pl.when(t < me)(lambda: push(1, t, c, t))

    def take(way, t, c):
        copy(way, t, c).wait_recv()
        out[c] += got[way, t, c].astype(jnp.float32)

    def finish():
        for c in range(pieces):
            out[c] = p[me, c].astype(jnp.float32)
        for t in range(n - 1):
            for c in range(pieces):
                pl.when((me > 0) & (n - 1 - t == me))(lambda: take(0, t, c))
                pl.when((me < n - 1) & (t == me))(lambda: take(1, t, c))
        for t in range(n - 1):
            for c in range(pieces):
                pl.when(n - 1 - t > me)(lambda: copy(0, t, c).wait_send())
                pl.when(t < me)(lambda: copy(1, t, c).wait_send())

    return [functools.partial(stage, t) for t in range(n - 1)] + [finish]


def pair_place(n):
    me = lax.axis_index("dp")
    core = lax.rem(me, 2)
    chip = (me - core) // 2
    twin = {"dp": me + 1 - 2 * core}
    return me, core, chip, twin


def group_gather(n, x, out, send, recv, fsend, frecv, own):
    me, core, chip, twin = pair_place(n)
    chips = n // 2

    def far(j):
        to = lax.rem(chip + j, chips) * 2 + core
        return remote(x, out.at[me], send.at[j], recv.at[j], {"dp": to})

    def source(j):
        return lax.rem(chip - j + chips, chips) * 2 + core

    def near(j):
        at = source(j)
        return remote(x if j == 0 else out.at[at], out.at[at], fsend.at[j], frecv.at[j], twin)

    def landed(j, at, sem_s, sem_r):
        remote(out.at[at], out.at[at], sem_s.at[j], sem_r.at[j], twin).wait_recv()

    def begin():
        for j in range(1, chips):
            far(j).start()
        near(0).start()
        pltpu.make_async_copy(x, out.at[me], own).start()

    def relay():
        for j in range(1, chips):
            landed(j, source(j), send, recv)
            near(j).start()

    def finish():
        for j in range(chips):
            landed(j, source(j) + 1 - 2 * core, fsend, frecv)
            near(j).wait_send()
        for j in range(1, chips):
            far(j).wait_send()
        pltpu.make_async_copy(x, out.at[me], own).wait()

    return [begin, relay, finish]


def group_scatter(n, g, out, tgot, both, fgot, send, recv, fsend, frecv):
    me, core, chip, twin = pair_place(n)
    chips = n // 2

    def near(j):
        to = lax.rem(chip + j, chips)
        return remote(g.at[to * 2 + 1 - core], tgot.at[j], fsend.at[j], frecv.at[j], twin)

    def far(j):
        to = lax.rem(chip + j, chips) * 2 + core
        return remote(both.at[j], fgot.at[j], send.at[j], recv.at[j], {"dp": to})

    order = list(range(1, chips)) + [0]

    def begin():
        for j in order:
            near(j).start()

    def spread():
        for j in order:
            near(j).wait_recv()
            mine = lax.rem(chip + j, chips) * 2 + core
            total = g[mine].astype(jnp.float32) + tgot[j].astype(jnp.float32)
            if j == 0:
                out[...] = total
            else:
                both[j] = total.astype(both.dtype)
                far(j).start()

    def finish():
        for j in range(1, chips):
            far(j).wait_recv()
            out[...] += fgot[j].astype(jnp.float32)
        for j in range(chips):
            near(j).wait_send()
        for j in range(1, chips):
            far(j).wait_send()

    return [begin, spread, finish]


def exchange(mesh, ident, gather=(), scatter=(), wide_gather=(), wide_scatter=()):
    n, m = mesh.shape["tensor"], mesh.shape["dp"]
    dma = pltpu.SemaphoreType.DMA
    vmem = pl.BlockSpec(memory_space=pltpu.VMEM)
    outs, specs, scratch, groups = [], [], [], []
    for x in gather:
        outs.append(jax.ShapeDtypeStruct((n,) + x.shape, x.dtype))
        specs.append(pl.BlockSpec(memory_space=pl.ANY))
        own = [dma((2, n - 1, x.shape[0])), dma((2, n - 1, x.shape[0])), dma]
        groups.append((functools.partial(line_gather, n, x.shape[0]), len(own)))
        scratch += own
    for x in scatter:
        outs.append(jax.ShapeDtypeStruct(x.shape[1:], jnp.float32))
        specs.append(vmem)
        slots = (2, n - 1) + x.shape[1:]
        own = [pltpu.VMEM(slots, x.dtype)] * 2 + [dma((2, n - 1, x.shape[1]))] * 2
        groups.append((functools.partial(line_scatter, n, x.shape[1]), len(own)))
        scratch += own
    for x in wide_gather:
        outs.append(jax.ShapeDtypeStruct((m,) + x.shape, x.dtype))
        specs.append(pl.BlockSpec(memory_space=pl.ANY))
        own = [dma((m // 2,))] * 4 + [dma]
        groups.append((functools.partial(group_gather, m), len(own)))
        scratch += own
    for x in wide_scatter:
        outs.append(jax.ShapeDtypeStruct(x.shape[1:], jnp.float32))
        specs.append(vmem)
        own = [pltpu.VMEM((m // 2,) + x.shape[1:], x.dtype)] * 3 + [dma((m // 2,))] * 4
        groups.append((functools.partial(group_scatter, m), len(own)))
        scratch += own
    operands = list(gather) + list(scatter) + list(wide_gather) + list(wide_scatter)
    count = len(operands)

    def kernel(*refs):
        ins, results, rest = refs[:count], refs[count:2 * count], list(refs[2 * count:])
        barrier = pltpu.get_barrier_semaphore()
        me = lax.axis_index("tensor")

        def greet(where):
            pl.semaphore_signal(barrier, inc=1, device_id=where, device_id_type=MESH_ID)

        if gather or scatter:
            pl.when(me > 0)(lambda: greet({"tensor": me - 1}))
            pl.when(me < n - 1)(lambda: greet({"tensor": me + 1}))
        if wide_gather or wide_scatter:
            _, core, chip, twin = pair_place(m)
            greet(twin)
            for j in range(1, m // 2):
                greet({"dp": lax.rem(chip + j, m // 2) * 2 + core})
        peers = m // 2 if wide_gather or wide_scatter else 0
        if gather or scatter:
            peers = peers + (me > 0).astype(jnp.int32) + (me < n - 1).astype(jnp.int32)
        pl.semaphore_wait(barrier, peers)
        plans = []
        for i, (make, size) in enumerate(groups):
            own, rest = rest[:size], rest[size:]
            plans.append(make(ins[i], results[i], *own))
        plans = plans[::-1]
        for row in itertools.zip_longest(*plans):
            for stage in row:
                if stage is not None:
                    stage()

    return pl.pallas_call(
        kernel, out_shape=tuple(outs), in_specs=[vmem] * count, out_specs=tuple(specs),
        scratch_shapes=scratch, name=f"exchange_{ident}",
        compiler_params=pltpu.CompilerParams(
            collective_id=ident, has_side_effects=True, vmem_limit_bytes=48 * 1024 * 1024),
    )(*operands)


PIECES = 2

def layer_norm(summed, gain, shift):
    center = summed - jnp.mean(summed, -1, keepdims=True)
    inv_std = lax.rsqrt(jnp.mean(center * center, -1, keepdims=True) + EPS)
    normed = center * inv_std
    return (normed * gain + shift, normed, inv_std)


def norm_back(upstream, normed, inv_std, gain):
    scaled = upstream * gain
    return inv_std * (
        scaled
        - jnp.mean(scaled, -1, keepdims=True)
        - normed * jnp.mean(scaled * normed, -1, keepdims=True)
    )


def gelu_parts(inputs):
    cdf_part = 0.5 * (1.0 + lax.erf(inputs * 0.7071067811865476))
    return (
        inputs * cdf_part,
        cdf_part + inputs * jnp.exp(-0.5 * inputs * inputs) * 0.3989422804014327,
    )


def local(
    mesh,
    tokens,
    segment_ids,
    qkv_weight,
    out_weight,
    in_weight,
    down_weight,
    qv_bias,
    hidden_bias,
    norm_vectors,
    cotangent,
):
    n, m = mesh.shape["tensor"], mesh.shape["dp"]
    seq_count, rows, width = tokens.shape
    share = qkv_weight.shape[1]
    part = qkv_weight.shape[2]
    hidden = in_weight.shape[1]
    qkv_cols = 3 * part
    marks = (qkv_cols, qkv_cols + part, qkv_cols + part + hidden)
    packed = jnp.concatenate(
        [qkv_weight[0], qkv_weight[1], qkv_weight[2], out_weight.T, in_weight, down_weight.T], axis=1
    )
    bias_len, hid_len = qv_bias.shape[2], hidden_bias.shape[1]
    vec_len = norm_vectors.shape[1]
    small = jnp.concatenate(
        [qv_bias.astype(jnp.float32).reshape(-1), hidden_bias.astype(jnp.float32).reshape(-1), norm_vectors.reshape(-1)]
    )
    small_len = small.shape[0]
    tile = -(-small_len // 1024) * 8
    small = jnp.pad(small, (0, tile * 128 - small_len)).reshape(tile, 128)

    def pieces_of(rows_in):
        return rows_in.reshape(PIECES, -1, width)

    def split(part_rows):
        return part_rows.astype(jnp.bfloat16).reshape(n, PIECES, -1, width)

    def whole(gathered):
        return gathered.reshape(seq_count, -1, width)

    tokens_all, packed_all, small_all = exchange(
        mesh, 1, gather=(pieces_of(tokens),), wide_gather=(packed, small)
    )
    full_tokens = whole(tokens_all)
    weights = packed_all.reshape(m * share, -1)
    qkv_full = weights[:, : marks[0]]
    out_full, in_full, down_full = (
        weights[:, marks[0] : marks[1]],
        weights[:, marks[1] : marks[2]],
        weights[:, marks[2] :],
    )
    small_all = small_all.reshape(m, -1)
    qv_full = small_all[:, : 2 * bias_len].reshape(m, 2, bias_len).transpose(1, 0, 2).reshape(2, -1)
    hidden_full = small_all[:, 2 * bias_len : 2 * bias_len + hid_len].reshape(-1)
    norm_here = small_all.reshape(1, -1, 128)
    length = full_tokens.shape[1]
    local_width = part
    heads_here = local_width // DH
    score_scale = DH ** (-0.5)
    block_rows = min(512, length)
    block_count = length // block_rows
    head_shape = (seq_count, length, heads_here, DH)
    flat = jnp.einsum("bld,de->ble", full_tokens, qkv_full, preferred_element_type=jnp.float32)
    projected = [flat[..., c * part : (c + 1) * part] for c in range(3)]
    queries = (projected[0] + qv_full[0]).astype(jnp.bfloat16).reshape(head_shape)
    key_rows = projected[1].astype(jnp.bfloat16).reshape(head_shape)
    value_rows = (projected[2] + qv_full[1]).astype(jnp.bfloat16).reshape(head_shape)

    def block_scores(block_index):
        row_start = block_index * block_rows
        query_block = lax.dynamic_slice_in_dim(queries, row_start, block_rows, 1)
        segment_block = lax.dynamic_slice_in_dim(segment_ids, row_start, block_rows, 1)
        scores = (
            jnp.einsum("bqhd,bkhd->bhqk", query_block, key_rows, preferred_element_type=jnp.float32)
            * score_scale
        )
        allowed = segment_block[:, None, :, None] == segment_ids[:, None, None, :]
        return (jnp.where(allowed, scores, MASKED), query_block)

    def attend(block_index):
        scores, query_block = block_scores(block_index)
        row_max = jnp.max(scores, -1, keepdims=True)
        shifted = jnp.exp(scores - row_max)
        row_total = jnp.sum(shifted, -1, keepdims=True)
        attn_probs = (shifted / row_total).astype(jnp.bfloat16)
        context = jnp.einsum(
            "bhqk,bkhd->bqhd", attn_probs, value_rows, preferred_element_type=jnp.float32
        ).astype(jnp.bfloat16)
        return (context, (row_max + jnp.log(row_total))[..., 0])

    contexts, log_sums = lax.map(attend, jnp.arange(block_count))
    context_rows = jnp.moveaxis(contexts, 0, 1).reshape(seq_count, length, local_width)
    attn_part = jnp.einsum(
        "ble,de->bld", context_rows, out_full, preferred_element_type=jnp.float32
    )
    norm_all, attn_sum = exchange(mesh, 2, gather=(norm_here,), scatter=(split(attn_part),))
    attn_sum = attn_sum.reshape(tokens.shape)
    norm_all = norm_all.reshape(n, m, -1)[:, :, 2 * bias_len + hid_len : small_len]
    vector_rows = norm_all.reshape(n, m, 6, vec_len).transpose(2, 1, 0, 3).reshape(6, -1)
    first_sum = tokens.astype(jnp.float32) + attn_sum + vector_rows[0]
    normed_one, unit_one, inv_one = layer_norm(first_sum, vector_rows[1], vector_rows[2])
    (normed_all,) = exchange(mesh, 3, gather=(pieces_of(normed_one.astype(jnp.bfloat16)),))
    normed_full = whole(normed_all)
    hidden_pre = (
        jnp.einsum("bld,df->blf", normed_full, in_full, preferred_element_type=jnp.float32)
        + hidden_full
    )
    activated, gelu_slope = gelu_parts(hidden_pre)
    act_low = activated.astype(jnp.bfloat16)
    mlp_part = jnp.einsum("blf,df->bld", act_low, down_full, preferred_element_type=jnp.float32)
    (mlp_sum,) = exchange(mesh, 4, scatter=(split(mlp_part),))
    mlp_sum = mlp_sum.reshape(tokens.shape)
    second_sum = normed_one + mlp_sum + vector_rows[3]
    normed_two, unit_two, inv_two = layer_norm(second_sum, vector_rows[4], vector_rows[5])
    layer_out = normed_two.astype(jnp.bfloat16)
    upstream = cotangent.astype(jnp.float32)
    grad_second = norm_back(upstream, unit_two, inv_two, vector_rows[4])
    (grad_mlp_all,) = exchange(mesh, 3, gather=(pieces_of(grad_second.astype(jnp.bfloat16)),))
    grad_mlp_full = whole(grad_mlp_all)
    down_grad = jnp.einsum(
        "bld,blf->df", grad_mlp_full, act_low, preferred_element_type=jnp.float32
    )
    grad_hidden = (
        jnp.einsum("bld,df->blf", grad_mlp_full, down_full, preferred_element_type=jnp.float32)
        * gelu_slope
    )
    hidden_low = grad_hidden.astype(jnp.bfloat16)
    hidden_grad = jnp.sum(grad_hidden, (0, 1))[None]
    in_grad = jnp.einsum("bld,blf->df", normed_full, hidden_low, preferred_element_type=jnp.float32)
    back_part = jnp.einsum("blf,df->bld", hidden_low, in_full, preferred_element_type=jnp.float32)
    (back_sum,) = exchange(mesh, 4, scatter=(split(back_part),))
    grad_normed = grad_second + back_sum.reshape(tokens.shape)
    grad_first = norm_back(grad_normed, unit_one, inv_one, vector_rows[1])
    vector_grad = jnp.stack(
        [
            jnp.sum(grad_first, (0, 1)),
            jnp.sum(grad_normed * unit_one, (0, 1)),
            jnp.sum(grad_normed, (0, 1)),
            jnp.sum(grad_second, (0, 1)),
            jnp.sum(upstream * unit_two, (0, 1)),
            jnp.sum(upstream, (0, 1)),
        ]
    )
    vector_tile = jnp.pad(vector_grad, ((0, 2), (0, 0)))[None]
    grad_attn_all, vector_all = exchange(
        mesh, 5, gather=(pieces_of(grad_first.astype(jnp.bfloat16)), vector_tile)
    )
    grad_attn_full = whole(grad_attn_all)
    vector_sum = jnp.sum(vector_all[:, 0, :6], 0).reshape(6, m, n, vec_len)
    vector_here = lax.dynamic_index_in_dim(vector_sum, lax.axis_index("tensor"), 2, keepdims=False)
    out_grad = jnp.einsum(
        "bld,ble->de", grad_attn_full, context_rows, preferred_element_type=jnp.float32
    )
    grad_context = jnp.einsum(
        "bld,de->ble", grad_attn_full, out_full, preferred_element_type=jnp.float32
    ).astype(jnp.bfloat16)
    grad_heads = grad_context.reshape(head_shape)
    row_delta = jnp.sum(
        grad_heads.astype(jnp.float32) * context_rows.reshape(head_shape).astype(jnp.float32), -1
    )

    def backward_block(running, block_index):
        key_grad, value_grad = running
        scores, query_block = block_scores(block_index)
        row_start = block_index * block_rows
        grad_block = lax.dynamic_slice_in_dim(grad_heads, row_start, block_rows, 1)
        delta_block = lax.dynamic_slice_in_dim(row_delta, row_start, block_rows, 1)
        probs_again = jnp.exp(scores - log_sums[block_index][..., None])
        probs_low = probs_again.astype(jnp.bfloat16)
        value_grad = value_grad + jnp.einsum(
            "bhqk,bqhd->bkhd", probs_low, grad_block, preferred_element_type=jnp.float32
        )
        grad_probs = jnp.einsum(
            "bqhd,bkhd->bhqk", grad_block, value_rows, preferred_element_type=jnp.float32
        )
        grad_scores = (
            probs_again * (grad_probs - jnp.transpose(delta_block, (0, 2, 1))[..., None])
        ).astype(jnp.bfloat16)
        query_grad = (
            jnp.einsum("bhqk,bkhd->bqhd", grad_scores, key_rows, preferred_element_type=jnp.float32)
            * score_scale
        )
        key_grad = (
            key_grad
            + jnp.einsum(
                "bhqk,bqhd->bkhd", grad_scores, query_block, preferred_element_type=jnp.float32
            )
            * score_scale
        )
        return ((key_grad, value_grad), query_grad)

    zero_heads = jnp.zeros(head_shape, jnp.float32)
    (key_grad, value_grad), query_grads = lax.scan(
        backward_block, (zero_heads, zero_heads), jnp.arange(block_count)
    )
    query_grad = jnp.moveaxis(query_grads, 0, 1).reshape(seq_count, length, local_width)
    key_grad = key_grad.reshape(seq_count, length, local_width)
    value_grad = value_grad.reshape(seq_count, length, local_width)
    bias_grad = jnp.stack([jnp.sum(query_grad, (0, 1)), jnp.sum(value_grad, (0, 1))])
    grads_low = jnp.concatenate([query_grad, key_grad, value_grad], -1).astype(jnp.bfloat16)
    qkv_grad = jnp.einsum("bld,ble->de", full_tokens, grads_low, preferred_element_type=jnp.float32)
    token_part = jnp.einsum("ble,de->bld", grads_low, qkv_full, preferred_element_type=jnp.float32)
    grads = jnp.concatenate(
        [g.astype(jnp.bfloat16) for g in (qkv_grad, out_grad, in_grad, down_grad)], axis=1
    ).reshape(m, share, -1)
    small_grads = jnp.concatenate(
        [
            bias_grad.reshape(2, m, bias_len).transpose(1, 0, 2).reshape(m, -1),
            hidden_grad.reshape(m, hid_len),
            vector_here.transpose(1, 0, 2).reshape(m, -1),
        ],
        axis=1,
    )
    small_grads = jnp.pad(small_grads, ((0, 0), (0, tile * 128 - small_len))).reshape(m, tile, 128)
    token_sum, grad_sum, small_sum = exchange(
        mesh, 6, scatter=(split(token_part),), wide_scatter=(grads, small_grads)
    )
    tokens_grad = (grad_first + token_sum.reshape(tokens.shape)).astype(jnp.bfloat16)
    qkv_shard = jnp.stack([grad_sum[:, c * part : (c + 1) * part] for c in range(3)])
    out_shard = grad_sum[:, marks[0] : marks[1]].T
    in_shard = grad_sum[:, marks[1] : marks[2]]
    down_shard = grad_sum[:, marks[2] :].T
    small_sum = small_sum.reshape(-1)
    bias_shard = small_sum[: 2 * bias_len].reshape(qv_bias.shape)
    hidden_shard = small_sum[2 * bias_len : 2 * bias_len + hid_len].reshape(hidden_bias.shape)
    vectors_grad = small_sum[2 * bias_len + hid_len : small_len].reshape(norm_vectors.shape)
    return (
        layer_out,
        tokens_grad,
        qkv_shard,
        out_shard,
        in_shard,
        down_shard,
        bias_shard,
        hidden_shard,
        vectors_grad,
    )


def solution(mesh):
    return jax.shard_map(
        functools.partial(local, mesh),
        mesh=mesh,
        in_specs=(
            P("dp", "tensor", None),
            P("dp", None),
            P(None, "dp", "tensor"),
            P("tensor", "dp"),
            P("dp", "tensor"),
            P("tensor", "dp"),
            P(None, "tensor", "dp"),
            P("tensor", "dp"),
            P(None, ("dp", "tensor")),
            P("dp", "tensor", None),
        ),
        out_specs=(
            P("dp", "tensor", None),
            P("dp", "tensor", None),
            P(None, "dp", "tensor"),
            P("tensor", "dp"),
            P("dp", "tensor"),
            P("tensor", "dp"),
            P(None, "tensor", "dp"),
            P("tensor", "dp"),
            P(None, ("dp", "tensor")),
        ),
        check_vma=False,
    )
```

time: 625 us -> 362 us (0.58)
  waiting for transfers between devices: 317 us -> 0 us
  Pallas kernels: 0 us -> 263 us
  blocking collectives: 162 us -> 0 us
  between operations: 17.5 us -> 1.45 us
  matrix products: 62.8 us -> 50.5 us
  other arithmetic: 25.1 us -> 15.2 us
    pallas_call x0 -> x8, Pallas kernels: none -> 263 us  [exchange(): pl.pallas_call(kernel, out_shape=tuple(outs), in_specs=[vmem] * count, ou...]
    reduce_scatter x6 -> x0, waiting for transfers between devices: 193 us -> none  [the longest x1 46.1 us: local(): lax.psum_scatter(in_grad, 'dp', scatter_dimension=0, tiled=True)]
    all_gather x6 -> x0, waiting for transfers between devices: 116 us -> none  [the longest x1 36.3 us: local(): lax.all_gather(grad_second.astype(jnp.bfloat16), 'tensor', axis=1, tiled=...]
    all_gather x4 -> x0, blocking collectives: 92.9 us -> none  [the longest x1 60.8 us: local(): lax.all_gather(norm_vectors, ('dp', 'tensor'), axis=1, tiled=True)]
    unnamed x3 -> x0, blocking collectives: 68.8 us -> none
    unnamed x77 -> x48, local copies, waits for them, and re-layouts: 21.6 us -> 5.33 us
    dot_general x8 -> x9, matrix products: 27 us -> 17.2 us  [the longest x1 2.81 us: local(): jnp.einsum('bld,df->blf', grad_mlp_full, down_full, preferred_element_typ...]
    unnamed x18 -> x0, waiting for transfers between devices: 7.39 us -> none
  transfers between devices with their start and end apart: 15 -> 0, of which waited for: 11 -> 0; matrix products, arithmetic and copies ran while one was open for 11% -> 0% of each run, Pallas kernels for 0% -> 0%
where the time goes in v1:
time: 362 us; the launch traced here: 361 us
  Pallas kernels  263 us (73%)
  matrix products  50.5 us (14%)
  local copies, waits for them, and re-layouts  24.9 us (7%)
  other arithmetic  15.2 us (4%)
  loops' own time  6.79 us (2%)
    pallas_call x8, Pallas kernels, exchange(): pl.pallas_call(kernel, out_shape=tuple(outs), in_specs=[vmem] * count, ou...  263 us

profile of v1, /device:TPU:10, one launch (start us, length us, event | category | flops | bytes accessed | tf_op | source)
XLA Modules:
  0.0 361.4 jit_solution(190510911004047034)
XLA Ops:
  3.4 0.9 copy.37
  4.3 0.9 slice_bitcast_fusion.5
  5.2 1.1 concatenate.27.refs_1_
  6.3 1.0 copy-done
  7.3 39.4 %exchange_1.1 = (bf16[4,2,128,768]{3,2,1,0:T(8,128)(2,1)S(1)}, bf16[8,96,2304]{2,1,0:T(8,128)(2,1)S(1)}, f32[8,8,128]{2,1,0:T(8,128)S(1)}) custom-call(bf16[2,128,768]{2,1,0:T(8,128)(2,1)S(1)} %bitcast.254, bf16[96,2304]{1,0:T(8,128)(2,1)S(1)} %concatenate.27.refs_1_, f32[8,128]{1,0:T(8,128)S(1)} %fusion.76.refs_2_), custom_call_target="tpu_custom_call" | custom-call | tf_op jit(solution)/shard_map/exchange_1/pallas_call | solution.py:255
  46.7 1.7 copy-done.2
  48.9 2.5 convolution_bitcast_fusion
  51.6 14.1 %while.27 = (s32[]{:T(128)}, bf16[2,1,512,3,64]{2,4,3,1,0:T(8,128)(2,1)S(1)}, f32[2,1,3,512]{3,2,1,0:T(4,128)S(1)}, s32[2]{0:T(128)S(1)}, s32[1,1024]{1,0:T(1,12...) while((s32[]{:T(128)}, ...), condition=%wide.region_3.4_spmd, body=%wide.region_0.3_spmd.sunk | while | flops 422148608 | bytes 22221000 | solution.py:380
  53.2 1.4 fusion.125
  54.6 1.8 fusion.126
  56.4 2.2 fusion.127
  60.3 1.4 fusion.125
  61.7 1.8 fusion.126
  63.5 2.2 fusion.127
  66.6 0.9 copy.51
  67.5 1.9 convolution_convert_fusion.3
  69.4 43.8 %exchange_2.1 = (f32[4,1,64,128]{3,2,1,0:T(8,128)S(1)}, f32[2,128,768]{2,1,0:T(8,128)S(1)}) custom-call(f32[1,64,128]{2,1,0:T(8,128)S(1)} %bitcast.275, bf16[4,2,128,768]{3,2,1,0:T(8,128)(2,1)S(1)} %bitcast.249), custom_call_target="tpu_custom_call" | custom-call | tf_op jit(solution)/shard_map/exchange_2/pallas_call | solution.py:255
  114.8 17.8 %exchange_3.2 = bf16[4,2,128,768]{3,2,1,0:T(8,128)(2,1)S(1)} custom-call(bf16[2,128,768]{2,1,0:T(8,128)(2,1)S(1)} %bitcast.261), custom_call_target="tpu_custom_call" | custom-call | tf_op jit(solution)/shard_map/exchange_3/pallas_call | solution.py:255
  132.7 4.0 %multiply_convert_fusion.1 = (bf16[1024,768]{1,0:T(8,128)(2,1)S(1)}, f32[1024,768]{1,0:T(8,128)S(1)}) fusion(f32[768]{0:T(1024)S(1)} %add.174, bf16[1024,768]{1,0:T(8,128)(2,1)S(1)} %bitcast.256, bf16[768,2304]{1,0:T(8,128)(2,1)S(1)} %bitcast.270), kind=kOutput, calls=%fused_computation.62 | convolution fusion | flops 1212678144 | bytes 7475200 | tf_op jit(solution)/shard_map/bld,df->blf/dot_general | solution.py:394
  136.6 1.4 convolution_convert_fusion.2
  138.1 38.9 %exchange_4.2 = f32[2,128,768]{2,1,0:T(8,128)S(1)} custom-call(bf16[4,2,128,768]{3,2,1,0:T(8,128)(2,1)S(1)} %bitcast.253), custom_call_target="tpu_custom_call" | custom-call | tf_op jit(solution)/shard_map/exchange_4/pallas_call | solution.py:255
  178.1 1.1 fusion.79
  179.2 15.7 %exchange_3.3 = bf16[4,2,128,768]{3,2,1,0:T(8,128)(2,1)S(1)} custom-call(bf16[2,128,768]{2,1,0:T(8,128)(2,1)S(1)} %bitcast.262), custom_call_target="tpu_custom_call" | custom-call | tf_op jit(solution)/shard_map/exchange_3/pallas_call | solution.py:255
  194.9 2.8 fusion.89
  197.7 2.4 convolution_convert_fusion.4
  200.1 2.6 convolution_convert_fusion.5
  203.4 3.2 convolution_convert_fusion.1
  206.6 36.1 %exchange_4.3 = f32[2,128,768]{2,1,0:T(8,128)S(1)} custom-call(bf16[4,2,128,768]{3,2,1,0:T(8,128)(2,1)S(1)} %bitcast.252), custom_call_target="tpu_custom_call" | custom-call | tf_op jit(solution)/shard_map/exchange_4/pallas_call | solution.py:255
  243.6 17.9 %exchange_5.1 = (bf16[4,2,128,768]{3,2,1,0:T(8,128)(2,1)S(1)}, f32[4,1,8,768]{3,2,1,0:T(8,128)S(1)}) custom-call(bf16[2,128,768]{2,1,0:T(8,128)(2,1)S(1)} %bitcast.255, f32[1,8,768]{2,1,0:T(8,128)S(1)} %pad_bitcast_fusion.refs_1_), custom_call_target="tpu_custom_call" | custom-call | tf_op jit(solution)/shard_map/exchange_5/pallas_call | solution.py:255
  261.9 1.8 convolution_convert_fusion.7
  264.0 23.9 %while.28 = (s32[]{:T(128)}, f32[1,1024,3,64]{1,3,2,0:T(8,128)S(1)}, f32[1,1024,3,64]{1,3,2,0:T(8,128)}, f32[2,1,512,3,64]{2,4,3,1,0:T(8,128)}, s32[2]{0:T(128)S...) while((s32[]{:T(128)}, ...), condition=%wide.region_20.21_spmd.clone, body=%wide.region_19.20_spmd.clone.sunk | while | flops 1023967232 | bytes 43313532 | solution.py:482
  267.6 1.0 fusion.138
  268.7 2.0 fusion.140
  270.7 2.6 multiply_convert_fusion.3
  273.3 0.8 fusion.139
  274.1 1.9 fusion.141
  279.6 1.0 fusion.138
  280.7 2.0 fusion.140
  282.7 2.6 multiply_convert_fusion.3
  286.0 1.8 fusion.141
  287.9 1.6 fusion.86
  290.5 2.8 convolution_convert_fusion
  293.3 1.1 convolution_convert_fusion.6
  295.0 2.1 pad_maximum_fusion
  297.0 5.8 %copy.47 = bf16[768,2304]{1,0:T(8,128)(2,1)} copy(bf16[768,2304]{0,1:T(8,128)(2,1)} %pad_maximum_fusion) | data formatting | bytes 7077888 | tf_op jit(solution)/shard_map/concatenate | solution.py:492
  303.1 53.0 %exchange_6.1 = (f32[2,128,768]{2,1,0:T(8,128)S(1)}, f32[96,2304]{1,0:T(8,128)S(1)}, f32[8,128]{1,0:T(8,128)S(1)}) custom-call(bf16[4,2,128,768]{3,2,1,0:T(8,128)(2,1)S(1)} %bitcast.258, bf16[8,96,2304]{2,1,0:T(8,128)(2,1)} %bitcast.283, f32[8,8,128]{2,1,0:T(8,128)S(1)} %bitcast.273), custom_call_target="tpu_custom_call" | custom-call | tf_op jit(solution)/shard_map/exchange_6/pallas_call | solution.py:255
  356.1 0.8 fusion.67
  359.0 0.9 slice_bitcast_fusion
  (162 shorter events, 19.0 us)
Async XLA Ops:
  6.3 1.0 copy-start
  46.7 1.8 copy-start.2
  48.4 3.0 copy-start.4
  48.9 2.7 copy-start.15
  65.7 0.7 copy-start.7
  65.7 3.6 %copy-start.19 = (bf16[1,1024,3,64]{1,3,2,0:T(8,128)(2,1)}, bf16[1,1024,3,64]{1,3,2,0:T(8,128)(2,1)S(1)}, u32[]{:S(2)}) copy-start(bf16[1,1024,3,64]{1,3,2,0:T(8,128)(2,1)S(1)} %get-tuple-element.514) | copy-start | bytes 1179652
  66.2 47.0 %copy-start.9 = (bf16[24,8,2,512]{3,1,2,0:T(8,128)(2,1)}, bf16[24,8,2,512]{3,1,2,0:T(8,128)(2,1)S(1)}, u32[]{:S(2)}) copy-start(bf16[24,8,2,512]{3,1,2,0:T(8,128)(2,1)S(1)} %copy.53) | copy-start | bytes 1179652
  66.6 47.6 %copy-start.1 = (bf16[1,256,768]{2,1,0:T(8,128)(2,1)S(1)}, bf16[1,256,768]{2,1,0:T(8,128)(2,1)}, u32[]{:S(2)}) copy-start(bf16[1,256,768]{2,1,0:T(8,128)(2,1)} %param.14) | copy-start | bytes 1179652
  114.2 18.5 %copy-start.3 = (bf16[8,96,2304]{2,1,0:T(8,128)(2,1)S(1)}, bf16[8,96,2304]{2,1,0:T(8,128)(2,1)}, u32[]{:S(2)}) copy-start(bf16[8,96,2304]{2,1,0:T(8,128)(2,1)} %copy-done.2) | copy-start | bytes 10616836
  138.1 39.5 %copy-start.12 = (bf16[1,256,768]{2,1,0:T(8,128)(2,1)S(1)}, bf16[1,256,768]{2,1,0:T(8,128)(2,1)}, u32[]{:S(2)}) copy-start(bf16[1,256,768]{2,1,0:T(8,128)(2,1)} %param.23) | copy-start | bytes 1179652
  197.7 2.5 copy-start.23
  242.6 18.8 %copy-start.10 = (bf16[24,8,2,512]{3,1,2,0:T(8,128)(2,1)S(1)}, bf16[24,8,2,512]{3,1,2,0:T(8,128)(2,1)}, u32[]{:S(2)}) copy-start(bf16[24,8,2,512]{3,1,2,0:T(8,128)(2,1)} %copy-done.9) | copy-start | bytes 1179652
  243.5 20.3 %copy-start.11 = (f32[2,1,3,8,8,512]{5,4,0,3,2,1:T(8,128)S(1)}, f32[2,1,3,8,8,512]{5,4,0,3,2,1:T(8,128)}, u32[]{:S(2)}) copy-start(f32[2,1,3,8,8,512]{5,4,0,3,2,1:T(8,128)} %copy.51) | copy-start | bytes 2359300
  243.5 20.4 %copy-start.6 = (f32[1,1024,3,64]{1,3,2,0:T(8,128)S(1)}, f32[1,1024,3,64]{1,3,2,0:T(8,128)}, u32[]{:S(2)}) copy-start(f32[1,1024,3,64]{1,3,2,0:T(8,128)} %custom-call) | copy-start | bytes 2359300
  243.5 20.4 %copy-start.8 = (bf16[1,1024,3,64]{1,3,2,0:T(8,128)(2,1)S(1)}, bf16[1,1024,3,64]{1,3,2,0:T(8,128)(2,1)}, u32[]{:S(2)}) copy-start(bf16[1,1024,3,64]{1,3,2,0:T(8,128)(2,1)} %copy-done.7) | copy-start | bytes 1179652
  243.6 20.4 %copy-start.22 = (s32[2]{0:T(128)S(1)}, s32[2]{0:T(128)}, u32[]{:S(2)}) copy-start(s32[2]{0:T(128)} %iota.7) | copy-start | bytes 28
  267.6 1.1 copy-start.16
  268.7 2.0 copy-start.20
  270.7 3.4 copy-start.17
  279.6 1.1 copy-start.16
  280.7 2.0 copy-start.20
  282.7 3.4 copy-start.17
  287.9 2.5 copy-start.18
  290.5 2.8 copy-start.5
  293.3 1.3 copy-start.13
  293.3 1.6 copy-start.14
  297.0 6.0 %copy-start.21 = (f32[8,96]{1,0:T(8,128)S(1)}, f32[8,96]{1,0:T(8,128)}, u32[]{:S(2)}) copy-start(f32[8,96]{1,0:T(8,128)} %reshape_broadcast_in_dim.3) | copy-start | bytes 9220

commit v2 on v1

--- a/solution.py
+++ b/solution.py
@@ -246,11 +246,15 @@
         for i, (make, size) in enumerate(groups):
             own, rest = rest[:size], rest[size:]
             plans.append(make(ins[i], results[i], *own))
-        plans = plans[::-1]
-        for row in itertools.zip_longest(*plans):
-            for stage in row:
-                if stage is not None:
-                    stage()
+        lines = plans[: len(gather) + len(scatter)][::-1]
+        wides = plans[len(lines) :][::-1]
+        run_stage = [lambda p=p: p[0]() for p in wides] + [lambda p=p: p[0]() for p in lines]
+        middle = [p[1] for p in wides]
+        along = [stage for row in itertools.zip_longest(*[p[1:-1] for p in lines]) for stage in row if stage]
+        run_stage += along[:-1] + middle + along[-1:] if wide_gather else middle + along
+        run_stage += [p[-1] for p in lines] + [p[-1] for p in wides]
+        for stage in run_stage:
+            stage()
 
     return pl.pallas_call(
         kernel, out_shape=tuple(outs), in_specs=[vmem] * count, out_specs=tuple(specs),

time: 362 us -> 346 us (0.956)
  Pallas kernels: 263 us -> 247 us
    pallas_call x8, Pallas kernels: 263 us -> 247 us  [exchange(): pl.pallas_call(kernel, out_shape=tuple(outs), in_specs=[vmem] * count, ou...]
where the time goes in v2:
time: 346 us
  Pallas kernels  247 us (71%)
  matrix products  50.5 us (15%)
  local copies, waits for them, and re-layouts  24.9 us (7%)
  other arithmetic  15.2 us (4%)
  loops' own time  6.79 us (2%)
    pallas_call x8, Pallas kernels, exchange(): pl.pallas_call(kernel, out_shape=tuple(outs), in_specs=[vmem] * count, ou...  247 us

profile of v2, /device:TPU:10, one launch (start us, length us, event | category | flops | bytes accessed | tf_op | source)
XLA Modules:
  0.0 345.5 jit_solution(9346100593630382292)
XLA Ops:
  3.4 0.9 copy.37
  4.3 0.9 slice_bitcast_fusion.5
  5.2 1.1 concatenate.27.refs_1_
  6.3 1.0 copy-done
  7.3 27.9 %exchange_1.1 = (bf16[4,2,128,768]{3,2,1,0:T(8,128)(2,1)S(1)}, bf16[8,96,2304]{2,1,0:T(8,128)(2,1)S(1)}, f32[8,8,128]{2,1,0:T(8,128)S(1)}) custom-call(bf16[2,128,768]{2,1,0:T(8,128)(2,1)S(1)} %bitcast.254, bf16[96,2304]{1,0:T(8,128)(2,1)S(1)} %concatenate.27.refs_1_, f32[8,128]{1,0:T(8,128)S(1)} %fusion.76.refs_2_), custom_call_target="tpu_custom_call" | custom-call | tf_op jit(solution)/shard_map/exchange_1/pallas_call | solution.py:259
  35.2 1.7 copy-done.2
  37.4 2.5 convolution_bitcast_fusion
  40.1 14.1 %while.27 = (s32[]{:T(128)}, bf16[2,1,512,3,64]{2,4,3,1,0:T(8,128)(2,1)S(1)}, f32[2,1,3,512]{3,2,1,0:T(4,128)S(1)}, s32[2]{0:T(128)S(1)}, s32[1,1024]{1,0:T(1,12...) while((s32[]{:T(128)}, ...), condition=%wide.region_3.4_spmd, body=%wide.region_0.3_spmd.sunk | while | flops 422148608 | bytes 22221000 | solution.py:384
  41.7 1.4 fusion.125
  43.1 1.8 fusion.126
  44.9 2.2 fusion.127
  48.8 1.4 fusion.125
  50.2 1.8 fusion.126
  52.0 2.2 fusion.127
  55.1 0.9 copy.51
  56.0 1.9 convolution_convert_fusion.3
  57.9 44.7 %exchange_2.1 = (f32[4,1,64,128]{3,2,1,0:T(8,128)S(1)}, f32[2,128,768]{2,1,0:T(8,128)S(1)}) custom-call(f32[1,64,128]{2,1,0:T(8,128)S(1)} %bitcast.275, bf16[4,2,128,768]{3,2,1,0:T(8,128)(2,1)S(1)} %bitcast.249), custom_call_target="tpu_custom_call" | custom-call | tf_op jit(solution)/shard_map/exchange_2/pallas_call | solution.py:259
  104.2 17.8 %exchange_3.2 = bf16[4,2,128,768]{3,2,1,0:T(8,128)(2,1)S(1)} custom-call(bf16[2,128,768]{2,1,0:T(8,128)(2,1)S(1)} %bitcast.261), custom_call_target="tpu_custom_call" | custom-call | tf_op jit(solution)/shard_map/exchange_3/pallas_call | solution.py:259
  122.0 4.0 %multiply_convert_fusion.1 = (bf16[1024,768]{1,0:T(8,128)(2,1)S(1)}, f32[1024,768]{1,0:T(8,128)S(1)}) fusion(f32[768]{0:T(1024)S(1)} %add.174, bf16[1024,768]{1,0:T(8,128)(2,1)S(1)} %bitcast.256, bf16[768,2304]{1,0:T(8,128)(2,1)S(1)} %bitcast.270), kind=kOutput, calls=%fused_computation.62 | convolution fusion | flops 1212678144 | bytes 7475200 | tf_op jit(solution)/shard_map/bld,df->blf/dot_general | solution.py:398
  126.0 1.4 convolution_convert_fusion.2
  127.4 38.9 %exchange_4.2 = f32[2,128,768]{2,1,0:T(8,128)S(1)} custom-call(bf16[4,2,128,768]{3,2,1,0:T(8,128)(2,1)S(1)} %bitcast.253), custom_call_target="tpu_custom_call" | custom-call | tf_op jit(solution)/shard_map/exchange_4/pallas_call | solution.py:259
  167.4 1.1 fusion.79
  168.6 15.7 %exchange_3.3 = bf16[4,2,128,768]{3,2,1,0:T(8,128)(2,1)S(1)} custom-call(bf16[2,128,768]{2,1,0:T(8,128)(2,1)S(1)} %bitcast.262), custom_call_target="tpu_custom_call" | custom-call | tf_op jit(solution)/shard_map/exchange_3/pallas_call | solution.py:259
  184.3 2.8 fusion.89
  187.1 2.4 convolution_convert_fusion.4
  189.5 2.6 convolution_convert_fusion.5
  192.8 3.2 convolution_convert_fusion.1
  196.0 36.0 %exchange_4.3 = f32[2,128,768]{2,1,0:T(8,128)S(1)} custom-call(bf16[4,2,128,768]{3,2,1,0:T(8,128)(2,1)S(1)} %bitcast.252), custom_call_target="tpu_custom_call" | custom-call | tf_op jit(solution)/shard_map/exchange_4/pallas_call | solution.py:259
  232.9 17.9 %exchange_5.1 = (bf16[4,2,128,768]{3,2,1,0:T(8,128)(2,1)S(1)}, f32[4,1,8,768]{3,2,1,0:T(8,128)S(1)}) custom-call(bf16[2,128,768]{2,1,0:T(8,128)(2,1)S(1)} %bitcast.255, f32[1,8,768]{2,1,0:T(8,128)S(1)} %pad_bitcast_fusion.refs_1_), custom_call_target="tpu_custom_call" | custom-call | tf_op jit(solution)/shard_map/exchange_5/pallas_call | solution.py:259
  251.3 1.8 convolution_convert_fusion.7
  253.4 23.9 %while.28 = (s32[]{:T(128)}, f32[1,1024,3,64]{1,3,2,0:T(8,128)S(1)}, f32[1,1024,3,64]{1,3,2,0:T(8,128)}, f32[2,1,512,3,64]{2,4,3,1,0:T(8,128)}, s32[2]{0:T(128)S...) while((s32[]{:T(128)}, ...), condition=%wide.region_20.21_spmd.clone, body=%wide.region_19.20_spmd.clone.sunk | while | flops 1023967232 | bytes 43313532 | solution.py:486
  257.0 1.0 fusion.138
  258.1 2.0 fusion.140
  260.1 2.6 multiply_convert_fusion.3
  262.7 0.8 fusion.139
  263.5 1.9 fusion.141
  268.9 1.0 fusion.138
  270.1 2.0 fusion.140
  272.1 2.6 multiply_convert_fusion.3
  275.4 1.8 fusion.141
  277.3 1.6 fusion.86
  279.9 2.8 convolution_convert_fusion
  282.7 1.1 convolution_convert_fusion.6
  284.3 2.1 pad_maximum_fusion
  286.4 5.8 %copy.47 = bf16[768,2304]{1,0:T(8,128)(2,1)} copy(bf16[768,2304]{0,1:T(8,128)(2,1)} %pad_maximum_fusion) | data formatting | bytes 7077888 | tf_op jit(solution)/shard_map/concatenate | solution.py:496
  292.5 47.8 %exchange_6.1 = (f32[2,128,768]{2,1,0:T(8,128)S(1)}, f32[96,2304]{1,0:T(8,128)S(1)}, f32[8,128]{1,0:T(8,128)S(1)}) custom-call(bf16[4,2,128,768]{3,2,1,0:T(8,128)(2,1)S(1)} %bitcast.258, bf16[8,96,2304]{2,1,0:T(8,128)(2,1)} %bitcast.283, f32[8,8,128]{2,1,0:T(8,128)S(1)} %bitcast.273), custom_call_target="tpu_custom_call" | custom-call | tf_op jit(solution)/shard_map/exchange_6/pallas_call | solution.py:259
  340.3 0.8 fusion.67
  343.2 0.9 slice_bitcast_fusion
  (162 shorter events, 19.0 us)
Async XLA Ops:
  6.3 1.0 copy-start
  35.2 1.8 copy-start.2
  36.9 3.0 copy-start.4
  37.4 2.7 copy-start.15
  54.2 0.7 copy-start.7
  54.2 3.6 %copy-start.19 = (bf16[1,1024,3,64]{1,3,2,0:T(8,128)(2,1)}, bf16[1,1024,3,64]{1,3,2,0:T(8,128)(2,1)S(1)}, u32[]{:S(2)}) copy-start(bf16[1,1024,3,64]{1,3,2,0:T(8,128)(2,1)S(1)} %get-tuple-element.514) | copy-start | bytes 1179652
  54.7 47.9 %copy-start.9 = (bf16[24,8,2,512]{3,1,2,0:T(8,128)(2,1)}, bf16[24,8,2,512]{3,1,2,0:T(8,128)(2,1)S(1)}, u32[]{:S(2)}) copy-start(bf16[24,8,2,512]{3,1,2,0:T(8,128)(2,1)S(1)} %copy.53) | copy-start | bytes 1179652
  55.1 48.5 %copy-start.1 = (bf16[1,256,768]{2,1,0:T(8,128)(2,1)S(1)}, bf16[1,256,768]{2,1,0:T(8,128)(2,1)}, u32[]{:S(2)}) copy-start(bf16[1,256,768]{2,1,0:T(8,128)(2,1)} %param.14) | copy-start | bytes 1179652
  103.6 18.5 %copy-start.3 = (bf16[8,96,2304]{2,1,0:T(8,128)(2,1)S(1)}, bf16[8,96,2304]{2,1,0:T(8,128)(2,1)}, u32[]{:S(2)}) copy-start(bf16[8,96,2304]{2,1,0:T(8,128)(2,1)} %copy-done.2) | copy-start | bytes 10616836
  127.4 39.6 %copy-start.12 = (bf16[1,256,768]{2,1,0:T(8,128)(2,1)S(1)}, bf16[1,256,768]{2,1,0:T(8,128)(2,1)}, u32[]{:S(2)}) copy-start(bf16[1,256,768]{2,1,0:T(8,128)(2,1)} %param.23) | copy-start | bytes 1179652
  187.1 2.5 copy-start.23
  232.0 18.8 %copy-start.10 = (bf16[24,8,2,512]{3,1,2,0:T(8,128)(2,1)S(1)}, bf16[24,8,2,512]{3,1,2,0:T(8,128)(2,1)}, u32[]{:S(2)}) copy-start(bf16[24,8,2,512]{3,1,2,0:T(8,128)(2,1)} %copy-done.9) | copy-start | bytes 1179652
  232.8 20.3 %copy-start.11 = (f32[2,1,3,8,8,512]{5,4,0,3,2,1:T(8,128)S(1)}, f32[2,1,3,8,8,512]{5,4,0,3,2,1:T(8,128)}, u32[]{:S(2)}) copy-start(f32[2,1,3,8,8,512]{5,4,0,3,2,1:T(8,128)} %copy.51) | copy-start | bytes 2359300
  232.9 20.4 %copy-start.6 = (f32[1,1024,3,64]{1,3,2,0:T(8,128)S(1)}, f32[1,1024,3,64]{1,3,2,0:T(8,128)}, u32[]{:S(2)}) copy-start(f32[1,1024,3,64]{1,3,2,0:T(8,128)} %custom-call) | copy-start | bytes 2359300
  232.9 20.4 %copy-start.8 = (bf16[1,1024,3,64]{1,3,2,0:T(8,128)(2,1)S(1)}, bf16[1,1024,3,64]{1,3,2,0:T(8,128)(2,1)}, u32[]{:S(2)}) copy-start(bf16[1,1024,3,64]{1,3,2,0:T(8,128)(2,1)} %copy-done.7) | copy-start | bytes 1179652
  232.9 20.4 %copy-start.22 = (s32[2]{0:T(128)S(1)}, s32[2]{0:T(128)}, u32[]{:S(2)}) copy-start(s32[2]{0:T(128)} %iota.7) | copy-start | bytes 28
  257.0 1.1 copy-start.16
  258.1 2.0 copy-start.20
  260.1 3.4 copy-start.17
  268.9 1.1 copy-start.16
  270.1 2.0 copy-start.20
  272.0 3.4 copy-start.17
  277.3 2.5 copy-start.18
  279.9 2.8 copy-start.5
  282.7 1.3 copy-start.13
  282.7 1.6 copy-start.14
  286.4 6.0 %copy-start.21 = (f32[8,96]{1,0:T(8,128)S(1)}, f32[8,96]{1,0:T(8,128)}, u32[]{:S(2)}) copy-start(f32[8,96]{1,0:T(8,128)} %reshape_broadcast_in_dim.3) | copy-start | bytes 9220
